TPU v7x, 32 devices: a whole 2x2x4 slice. The times are simulated.
32 devices in a mesh: row: 4 (over y, x), seq: 8 (over z, core).
Axes of the slice: x: 2, y: 2, z: 4, core: 2. Of those that a mesh axis runs over, the one named last changes fastest.
Arguments:
- hidden_in: bfloat16 [4, 1024, 2048], P('row', 'seq'), may hold values from -6 to 6
- positions: int32 [4, 1024], P('row', 'seq'), may hold values from 0 to 7164, as said below
- languages: int32 [4], replicated, may hold values from 0 to 6
- ln1_gain: bfloat16 [2048], replicated, may hold values from 0.5 to 1.5
- ln1_bias: bfloat16 [2048], replicated, may hold values from -1.1953125 to 1.1953125
- w_qkv: bfloat16 [2048, 6144], P(None, 'seq'), may hold values from -0.125 to 0.125
- b_qkv: bfloat16 [6144], P('seq'), may hold values from -1.1953125 to 1.1953125
- w_out: bfloat16 [2048, 2048], P('seq'), may hold values from -3 to 3
- ln2_gain: bfloat16 [2048], replicated, may hold values from 0.5 to 1.5
- ln2_bias: bfloat16 [2048], replicated, may hold values from -1.1953125 to 1.1953125
- w_gate: bfloat16 [2048, 5632], P(None, 'seq'), may hold values from -0.125 to 0.125
- w_up: bfloat16 [2048, 5632], P(None, 'seq'), may hold values from -0.125 to 0.125
- w_down: bfloat16 [5632, 2048], P('seq'), may hold values from -0.078125 to 0.078125
- cotangent: bfloat16 [4, 1024, 2048], P('row', 'seq'), may hold values from -6 to 6
Outputs:
- output: bfloat16 [4, 1024, 2048], P('row', 'seq')
- input_grad: bfloat16 [4, 1024, 2048], P('row', 'seq')
- grad_ln1_gain: float32 [2048], P('seq')
- grad_ln1_bias: float32 [2048], P('seq')
- grad_w_qkv: float32 [2048, 6144], P(None, 'seq')
- grad_b_qkv: float32 [6144], P('seq')
- grad_w_out: float32 [2048, 2048], P('seq')
- grad_ln2_gain: float32 [2048], P('seq')
- grad_ln2_bias: float32 [2048], P('seq')
- grad_w_gate: float32 [2048, 5632], P(None, 'seq')
- grad_w_up: float32 [2048, 5632], P(None, 'seq')
- grad_w_down: float32 [5632, 2048], P('seq')
Inputs may be any that keep to these rules, and one draw needn't show every extreme that they name: Each sequence's positions start at an offset of 0 to 4095 and rise by 1 to 3 from one token to the next; some sequence starts at 0, and another starts at 4095 and rises by 3 at every token.
All inputs are finite; a program needn't handle non-finite values.
Results may differ from a plain program's by a relative error of at most 0.013.
Values may be sent and summed in bfloat16 or wider, within the bound.
No kernel may reach another device: no remote copies, remote signals or barrier semaphores. Data moves between devices by JAX's collectives and lax.ppermute only.
A program may use at most 256 MiB of HBM per device.

v0:
```python
import jax
import jax.numpy as jnp
from jax import lax
from jax.sharding import PartitionSpec as P

HEAD_DIM = 64
ROT = 16
LANGS = 7
EPS = 1e-05
NEG = -1e30
BASE = 10000.0


def rotate(tensor, places, direction):
    half_rot = ROT // 2
    freqs = BASE ** (-(jnp.arange(half_rot, dtype=jnp.float32) * 2.0) / ROT)
    angles = places.astype(jnp.float32)[:, None] * freqs[None, :]
    cosine = jnp.cos(angles)[:, None, :]
    sine = jnp.sin(angles)[:, None, :] * direction
    first_half = tensor[..., :half_rot]
    second_half = tensor[..., half_rot:ROT]
    return jnp.concatenate(
        [
            first_half * cosine - second_half * sine,
            second_half * cosine + first_half * sine,
            tensor[..., ROT:],
        ],
        axis=-1,
    )


def standardize(values):
    center = values - jnp.mean(values, -1, keepdims=True)
    spread = jnp.mean(center * center, -1, keepdims=True)
    inverse = lax.rsqrt(spread + EPS)
    return (center * inverse, inverse)


def norm_back(grad_normed, normed, inverse):
    return inverse * (
        grad_normed
        - jnp.mean(grad_normed, -1, keepdims=True)
        - normed * jnp.mean(grad_normed * normed, -1, keepdims=True)
    )


def left_outer(left, right):
    return lax.dot_general(
        left, right, (((0,), (0,)), ((), ())), preferred_element_type=jnp.float32
    )


def right_outer(left, right):
    return lax.dot_general(
        left, right, (((1,), (1,)), ((), ())), preferred_element_type=jnp.float32
    )


def head_scores(query_part, key_part, query_ids, key_ids, factor):
    logits = (
        jnp.einsum("qhd,khd->hqk", query_part, key_part, preferred_element_type=jnp.float32)
        * factor
    )
    return jnp.where(key_ids[None, None, :] <= query_ids[None, :, None], logits, NEG)


def body(
    hidden_in,
    positions,
    languages,
    ln1_gain,
    ln1_bias,
    w_qkv,
    b_qkv,
    w_out,
    ln2_gain,
    ln2_bias,
    w_gate,
    w_up,
    w_down,
    cotangent,
):
    tokens = hidden_in[0].astype(jnp.float32)
    places = positions[0]
    shard_rows = tokens.shape[0]
    width = tokens.shape[1]
    seq_devices = lax.axis_size("seq")
    length = shard_rows * seq_devices
    position_here = lax.axis_index("seq")
    heads_count = width // HEAD_DIM
    group_heads = 4
    group_steps = heads_count // group_heads
    group_width = group_heads * HEAD_DIM
    factor = float(HEAD_DIM) ** (-0.5)
    language_ids = jnp.arange(LANGS, dtype=jnp.int32)
    marks_all = (languages[:, None] == language_ids[None, :]).astype(jnp.int32)
    language_totals = jnp.sum(marks_all, 0)
    own_language = lax.dynamic_slice_in_dim(languages, lax.axis_index("row"), 1, 0)
    own_marks = (own_language[0] == language_ids).astype(jnp.int32)
    own_count = jnp.sum(own_marks * language_totals)
    row_weight = jnp.float32(languages.shape[0] * length) / (
        LANGS * (own_count * length).astype(jnp.float32)
    )
    gain_one = ln1_gain.astype(jnp.float32)
    shift_one = ln1_bias.astype(jnp.float32)
    gain_two = ln2_gain.astype(jnp.float32)
    shift_two = ln2_bias.astype(jnp.float32)
    normed_one, inverse_one = standardize(tokens)
    first_in = (normed_one * gain_one + shift_one).astype(jnp.bfloat16)
    qkv_full, out_full, bias_full = (
        lax.all_gather(w_qkv, "seq", axis=1, tiled=True),
        lax.all_gather(w_out, "seq", axis=0, tiled=True),
        lax.all_gather(b_qkv, "seq", axis=0, tiled=True),
    )
    projected = jnp.dot(first_in, qkv_full, preferred_element_type=jnp.float32) + bias_full.astype(
        jnp.float32
    )
    head_shape = (shard_rows, heads_count, HEAD_DIM)
    queries = (
        rotate(projected[:, :width].reshape(head_shape), places, 1.0)
        .reshape(shard_rows, width)
        .astype(jnp.bfloat16)
    )
    keys_local = (
        rotate(projected[:, width : 2 * width].reshape(head_shape), places, 1.0)
        .reshape(shard_rows, width)
        .astype(jnp.bfloat16)
    )
    values_local = projected[:, 2 * width :].astype(jnp.bfloat16)
    keys_full, values_full = (
        lax.all_gather(keys_local, "seq", axis=0, tiled=True),
        lax.all_gather(values_local, "seq", axis=0, tiled=True),
    )
    query_ids = position_here * shard_rows + jnp.arange(shard_rows, dtype=jnp.int32)
    key_ids = jnp.arange(length, dtype=jnp.int32)

    def split_heads(matrix, column):
        return lax.dynamic_slice_in_dim(matrix, column, group_width, 1).reshape(
            matrix.shape[0], group_heads, HEAD_DIM
        )

    def attend_forward(number, carry):
        mixed_acc, stats = carry
        column = number * group_width
        logits = head_scores(
            split_heads(queries, column), split_heads(keys_full, column), query_ids, key_ids, factor
        )
        peak = jnp.max(logits, -1, keepdims=True)
        expo = jnp.exp(logits - peak)
        denom = jnp.sum(expo, -1, keepdims=True)
        probs = (expo / denom).astype(jnp.bfloat16)
        mixed_part = jnp.einsum(
            "hqk,khd->qhd",
            probs,
            split_heads(values_full, column),
            preferred_element_type=jnp.float32,
        )
        mixed_acc = lax.dynamic_update_slice_in_dim(
            mixed_acc, mixed_part.reshape(shard_rows, group_width), column, 1
        )
        stats = lax.dynamic_update_slice_in_dim(
            stats, (peak + jnp.log(denom))[..., 0], number * group_heads, 0
        )
        return (mixed_acc, stats)

    mixed_f, log_sums = lax.fori_loop(
        0,
        group_steps,
        attend_forward,
        (
            jnp.zeros((shard_rows, width), jnp.float32),
            jnp.zeros((heads_count, shard_rows), jnp.float32),
        ),
    )
    mixed = mixed_f.astype(jnp.bfloat16)
    middle = tokens + jnp.dot(mixed, out_full, preferred_element_type=jnp.float32)
    normed_two, inverse_two = standardize(middle)
    second_in = (normed_two * gain_two + shift_two).astype(jnp.bfloat16)
    second_full = lax.all_gather(second_in, "seq", axis=0, tiled=True)
    gate = jnp.dot(second_full, w_gate, preferred_element_type=jnp.float32)
    upward = jnp.dot(second_full, w_up, preferred_element_type=jnp.float32)
    sigmoid_gate = jax.nn.sigmoid(gate)
    activated = gate * sigmoid_gate
    hidden = (activated * upward).astype(jnp.bfloat16)
    feed_out = lax.psum_scatter(
        jnp.dot(hidden, w_down, preferred_element_type=jnp.float32).astype(jnp.bfloat16),
        "seq",
        scatter_dimension=0,
        tiled=True,
    ).astype(jnp.float32)
    output = (middle + feed_out).astype(jnp.bfloat16)[None]
    grad_top = cotangent[0].astype(jnp.float32) * row_weight
    grad_top_low = grad_top.astype(jnp.bfloat16)
    grad_top_full = lax.all_gather(grad_top_low, "seq", axis=0, tiled=True)
    grad_hidden = right_outer(grad_top_full, w_down)
    grad_w_down = left_outer(hidden, grad_top_full)
    slope = sigmoid_gate * (1.0 + gate * (1.0 - sigmoid_gate))
    grad_gate = (grad_hidden * upward * slope).astype(jnp.bfloat16)
    grad_upward = (grad_hidden * activated).astype(jnp.bfloat16)
    grad_w_gate = left_outer(second_full, grad_gate)
    grad_w_up = left_outer(second_full, grad_upward)
    grad_second = lax.psum_scatter(
        right_outer(grad_gate, w_gate) + right_outer(grad_upward, w_up),
        "seq",
        scatter_dimension=0,
        tiled=True,
    )
    grad_ln2_gain = jnp.sum(grad_second * normed_two, 0)
    grad_ln2_bias = jnp.sum(grad_second, 0)
    grad_middle = grad_top + norm_back(grad_second * gain_two, normed_two, inverse_two)
    grad_middle_low = grad_middle.astype(jnp.bfloat16)
    grad_w_out = left_outer(mixed, grad_middle_low)
    grad_mixed = right_outer(grad_middle_low, out_full).astype(jnp.bfloat16)

    def attend_back(number, carry):
        grad_query_acc, grad_key_acc, grad_value_acc = carry
        column = number * group_width
        query_part = split_heads(queries, column)
        key_part = split_heads(keys_full, column)
        grad_part = split_heads(grad_mixed, column)
        stats = lax.dynamic_slice_in_dim(log_sums, number * group_heads, group_heads, 0)
        logits = head_scores(query_part, key_part, query_ids, key_ids, factor)
        probs = jnp.exp(logits - stats[:, :, None])
        grad_probs = jnp.einsum(
            "qhd,khd->hqk",
            grad_part,
            split_heads(values_full, column),
            preferred_element_type=jnp.float32,
        )
        grad_values = jnp.einsum(
            "hqk,qhd->khd",
            probs.astype(jnp.bfloat16),
            grad_part,
            preferred_element_type=jnp.float32,
        )
        inner = jnp.sum(grad_probs * probs, -1, keepdims=True)
        grad_logits = (probs * (grad_probs - inner)).astype(jnp.bfloat16)
        grad_queries = (
            jnp.einsum("hqk,khd->qhd", grad_logits, key_part, preferred_element_type=jnp.float32)
            * factor
        )
        grad_keys = (
            jnp.einsum("hqk,qhd->khd", grad_logits, query_part, preferred_element_type=jnp.float32)
            * factor
        )
        key_sum, value_sum = (
            lax.psum_scatter(
                grad_keys.reshape(length, group_width), "seq", scatter_dimension=0, tiled=True
            ),
            lax.psum_scatter(
                grad_values.reshape(length, group_width), "seq", scatter_dimension=0, tiled=True
            ),
        )
        grad_query_acc = lax.dynamic_update_slice_in_dim(
            grad_query_acc, grad_queries.reshape(shard_rows, group_width), column, 1
        )
        grad_key_acc = lax.dynamic_update_slice_in_dim(grad_key_acc, key_sum, column, 1)
        grad_value_acc = lax.dynamic_update_slice_in_dim(grad_value_acc, value_sum, column, 1)
        return (grad_query_acc, grad_key_acc, grad_value_acc)

    empty = jnp.zeros((shard_rows, width), jnp.float32)
    grad_query_all, grad_key_all, grad_value_all = lax.fori_loop(
        0, group_steps, attend_back, (empty, empty, empty)
    )
    grad_query_turned = rotate(grad_query_all.reshape(head_shape), places, -1.0).reshape(
        shard_rows, width
    )
    grad_key_turned = rotate(grad_key_all.reshape(head_shape), places, -1.0).reshape(
        shard_rows, width
    )
    grad_projected = jnp.concatenate(
        [grad_query_turned, grad_key_turned, grad_value_all], 1
    ).astype(jnp.bfloat16)
    grad_w_qkv = left_outer(first_in, grad_projected)
    grad_b_qkv = jnp.sum(grad_projected.astype(jnp.float32), 0)
    grad_first = right_outer(grad_projected, qkv_full)
    grad_ln1_gain = jnp.sum(grad_first * normed_one, 0)
    grad_ln1_bias = jnp.sum(grad_first, 0)
    input_grad = (grad_middle + norm_back(grad_first * gain_one, normed_one, inverse_one)).astype(
        jnp.bfloat16
    )[None]
    seq_sums = (
        lax.psum_scatter(grad_ln1_gain, "seq", scatter_dimension=0, tiled=True),
        lax.psum_scatter(grad_ln1_bias, "seq", scatter_dimension=0, tiled=True),
        lax.psum_scatter(grad_w_qkv, "seq", scatter_dimension=1, tiled=True),
        lax.psum_scatter(grad_b_qkv, "seq", scatter_dimension=0, tiled=True),
        lax.psum_scatter(grad_w_out, "seq", scatter_dimension=0, tiled=True),
        lax.psum_scatter(grad_ln2_gain, "seq", scatter_dimension=0, tiled=True),
        lax.psum_scatter(grad_ln2_bias, "seq", scatter_dimension=0, tiled=True),
    )
    totals = lax.psum(
        (
            seq_sums[0],
            seq_sums[1],
            seq_sums[2],
            seq_sums[3],
            seq_sums[4],
            seq_sums[5],
            seq_sums[6],
            grad_w_gate,
            grad_w_up,
            grad_w_down,
        ),
        "row",
    )
    return (
        output,
        input_grad,
        totals[0],
        totals[1],
        totals[2],
        totals[3],
        totals[4],
        totals[5],
        totals[6],
        totals[7],
        totals[8],
        totals[9],
    )


def solution(mesh):
    placed = (
        P("row", "seq", None),
        P("row", "seq"),
        P(),
        P(),
        P(),
        P(None, "seq"),
        P("seq"),
        P("seq", None),
        P(),
        P(),
        P(None, "seq"),
        P(None, "seq"),
        P("seq", None),
        P("row", "seq", None),
    )
    return jax.shard_map(
        body,
        mesh=mesh,
        in_specs=placed,
        out_specs=(
            P("row", "seq", None),
            P("row", "seq", None),
            P("seq"),
            P("seq"),
            P(None, "seq"),
            P("seq"),
            P("seq", None),
            P("seq"),
            P("seq"),
            P(None, "seq"),
            P(None, "seq"),
            P("seq", None),
        ),
        check_vma=False,
    )
```

profile of v0, /device:TPU:0, one launch (start us, length us, event | category | flops | bytes accessed | tf_op | source)
XLA Modules:
  0.0 2399.7 jit_solution(3810746980370201801)
XLA Ops:
  8.0 15.8 all-gather
  24.4 207.9 %all-gather.8.cloned.1.call-done = bf16[2048,6144]{1,0:T(8,128)(2,1)} async-done(((bf16[2048,768]{1,0:T(8,128)(2,1)}), bf16[2048,6144]{1,0:T(8,128)(2,1)}) %all-gather.8.cloned.1.call-update) | async-done | bytes 25165840 | tf_op jit(solution)/shard_map/all_gather | solution.py:111
  232.3 10.1 convolution_add_fusion
  263.6 26.6 %all-gather.10.cloned.1.call-done = bf16[1024,2048]{1,0:T(8,128)(2,1)} async-done(((bf16[128,2048]{1,0:T(8,128)(2,1)}), bf16[1024,2048]{1,0:T(8,128)(2,1)}) %all-gather.10.cloned.1.call-update) | async-done | bytes 4194320 | tf_op jit(solution)/shard_map/all_gather | solution.py:132
  290.1 6.4 copy.55
  296.5 42.4 %all-gather.12.cloned.1.call-done = bf16[1024,2048]{0,1:T(8,128)(2,1)} async-done(((bf16[128,2048]{0,1:T(8,128)(2,1)}), bf16[1024,2048]{0,1:T(8,128)(2,1)}) %all-gather.12.cloned.1.call-update) | async-done | bytes 4194320 | tf_op jit(solution)/shard_map/all_gather | solution.py:131
  339.0 39.6 %while.34 = (s32[]{:T(128)}, bf16[128,2048]{0,1:T(8,128)(2,1)}, f32[32,128]{1,0:T(8,128)S(1)}, bf16[1024,2048]{0,1:T(8,128)(2,1)}, bf16[128,2048]{0,1:T(8,128)(2...) while((s32[]{:T(128)}, bf16[128,2048]{0,1:T(8,128)(2,1)}, ...), condition=%wide.region_5.0_spmd.clone, body=%wide.region_2.5_spmd.clone.sunk | while | flops 140639872 | bytes 10372341 | solution.py:166
  378.6 42.1 %all-gather.14.cloned.1.call-done = bf16[2048,2048]{1,0:T(8,128)(2,1)} async-done(((bf16[256,2048]{1,0:T(8,128)(2,1)}), bf16[2048,2048]{1,0:T(8,128)(2,1)}) %all-gather.14.cloned.1.call-update) | async-done | bytes 8388624 | tf_op jit(solution)/shard_map/all_gather | solution.py:112
  420.7 4.9 fusion.46
  431.9 41.3 %all-gather.16.cloned.1.call-done = bf16[1024,2048]{1,0:T(8,128)(2,1)} async-done(((bf16[128,2048]{1,0:T(8,128)(2,1)}), bf16[1024,2048]{1,0:T(8,128)(2,1)}) %all-gather.16.cloned.1.call-update) | async-done | bytes 4194320 | tf_op jit(solution)/shard_map/all_gather | solution.py:179
  473.3 8.0 fusion.47
  481.2 4.8 fusion.48
  486.0 35.0 %all-gather.18.cloned.1.call-done = bf16[1024,2048]{1,0:T(8,128)(2,1)} async-done(((bf16[128,2048]{1,0:T(8,128)(2,1)}), bf16[1024,2048]{1,0:T(8,128)(2,1)}) %all-gather.18.cloned.1.call-update) | async-done | bytes 4194320 | tf_op jit(solution)/shard_map/all_gather | solution.py:194
  521.0 8.6 multiply_convert_fusion.1
  533.1 6.0 convolution_add_fusion.1
  539.2 6.6 convolution_convert_fusion
  545.9 81.8 %reduce-scatter.9.cloned.1.call-done = f32[128,2048]{1,0:T(8,128)} async-done(((f32[1024,2048]{1,0:T(8,128)}), f32[128,2048]{1,0:T(8,128)}) %reduce-scatter.9.cloned.1.call-update) | async-done | bytes 1048592 | tf_op jit(solution)/shard_map/reduce_scatter | solution.py:202
  629.3 49.6 %reduce-scatter.7.cloned.1.call-done = bf16[128,2048]{1,0:T(8,128)(2,1)} async-done(((bf16[1024,2048]{1,0:T(8,128)(2,1)}), bf16[128,2048]{1,0:T(8,128)(2,1)}) %reduce-scatter.7.cloned.1.call-update) | async-done | bytes 524304 | tf_op jit(solution)/shard_map/reduce_scatter | solution.py:185
  681.7 9.4 fusion.34
  691.2 6.3 convolution_convert_fusion.1
  699.6 566.8 %while.35 = (s32[]{:T(128)}, f32[128,2048]{0,1:T(8,128)}, f32[128,2048]{0,1:T(8,128)}, bf16[128,2048]{0,1:T(8,128)(2,1)}, bf16[1024,2048]{0,1:T(8,128)(2,1)}, /*...) while((s32[]{:T(128)}, f32[128,2048]{0,1:T(8,128)}, ...), condition=%wide.region_18.0_spmd.clone, body=%wide.region_14.18_spmd.clone.sunk | while | flops 340688512 | bytes 36711860 | solution.py:262
  708.6 27.6 %reduce-scatter.15.cloned.1.call-done = f32[128,256]{0,1:T(8,128)} async-done(((f32[1024,256]{0,1:T(8,128)}), f32[128,256]{0,1:T(8,128)}) %reduce-scatter.15.cloned.1.call-update) | async-done | bytes 131088 | tf_op jit(solution)/shard_map/while/body/eval_jaxpr/reduce_scatter | solution.py:247
  737.8 31.3 %reduce-scatter.17.cloned.1.call-done = f32[128,256]{0,1:T(8,128)} async-done(((f32[1024,256]{0,1:T(8,128)}), f32[128,256]{0,1:T(8,128)}) %reduce-scatter.17.cloned.1.call-update) | async-done | bytes 131088 | tf_op jit(solution)/shard_map/while/body/eval_jaxpr/reduce_scatter | solution.py:250
  779.6 27.4 %reduce-scatter.15.cloned.1.call-done = f32[128,256]{0,1:T(8,128)} async-done(((f32[1024,256]{0,1:T(8,128)}), f32[128,256]{0,1:T(8,128)}) %reduce-scatter.15.cloned.1.call-update) | async-done | bytes 131088 | tf_op jit(solution)/shard_map/while/body/eval_jaxpr/reduce_scatter | solution.py:247
  808.6 31.3 %reduce-scatter.17.cloned.1.call-done = f32[128,256]{0,1:T(8,128)} async-done(((f32[1024,256]{0,1:T(8,128)}), f32[128,256]{0,1:T(8,128)}) %reduce-scatter.17.cloned.1.call-update) | async-done | bytes 131088 | tf_op jit(solution)/shard_map/while/body/eval_jaxpr/reduce_scatter | solution.py:250
  850.4 27.3 %reduce-scatter.15.cloned.1.call-done = f32[128,256]{0,1:T(8,128)} async-done(((f32[1024,256]{0,1:T(8,128)}), f32[128,256]{0,1:T(8,128)}) %reduce-scatter.15.cloned.1.call-update) | async-done | bytes 131088 | tf_op jit(solution)/shard_map/while/body/eval_jaxpr/reduce_scatter | solution.py:247
  879.3 31.4 %reduce-scatter.17.cloned.1.call-done = f32[128,256]{0,1:T(8,128)} async-done(((f32[1024,256]{0,1:T(8,128)}), f32[128,256]{0,1:T(8,128)}) %reduce-scatter.17.cloned.1.call-update) | async-done | bytes 131088 | tf_op jit(solution)/shard_map/while/body/eval_jaxpr/reduce_scatter | solution.py:250
  921.2 27.3 %reduce-scatter.15.cloned.1.call-done = f32[128,256]{0,1:T(8,128)} async-done(((f32[1024,256]{0,1:T(8,128)}), f32[128,256]{0,1:T(8,128)}) %reduce-scatter.15.cloned.1.call-update) | async-done | bytes 131088 | tf_op jit(solution)/shard_map/while/body/eval_jaxpr/reduce_scatter | solution.py:247
  950.1 31.4 %reduce-scatter.17.cloned.1.call-done = f32[128,256]{0,1:T(8,128)} async-done(((f32[1024,256]{0,1:T(8,128)}), f32[128,256]{0,1:T(8,128)}) %reduce-scatter.17.cloned.1.call-update) | async-done | bytes 131088 | tf_op jit(solution)/shard_map/while/body/eval_jaxpr/reduce_scatter | solution.py:250
  992.0 27.3 %reduce-scatter.15.cloned.1.call-done = f32[128,256]{0,1:T(8,128)} async-done(((f32[1024,256]{0,1:T(8,128)}), f32[128,256]{0,1:T(8,128)}) %reduce-scatter.15.cloned.1.call-update) | async-done | bytes 131088 | tf_op jit(solution)/shard_map/while/body/eval_jaxpr/reduce_scatter | solution.py:247
  1020.8 31.4 %reduce-scatter.17.cloned.1.call-done = f32[128,256]{0,1:T(8,128)} async-done(((f32[1024,256]{0,1:T(8,128)}), f32[128,256]{0,1:T(8,128)}) %reduce-scatter.17.cloned.1.call-update) | async-done | bytes 131088 | tf_op jit(solution)/shard_map/while/body/eval_jaxpr/reduce_scatter | solution.py:250
  1062.7 27.4 %reduce-scatter.15.cloned.1.call-done = f32[128,256]{0,1:T(8,128)} async-done(((f32[1024,256]{0,1:T(8,128)}), f32[128,256]{0,1:T(8,128)}) %reduce-scatter.15.cloned.1.call-update) | async-done | bytes 131088 | tf_op jit(solution)/shard_map/while/body/eval_jaxpr/reduce_scatter | solution.py:247
  1091.7 31.3 %reduce-scatter.17.cloned.1.call-done = f32[128,256]{0,1:T(8,128)} async-done(((f32[1024,256]{0,1:T(8,128)}), f32[128,256]{0,1:T(8,128)}) %reduce-scatter.17.cloned.1.call-update) | async-done | bytes 131088 | tf_op jit(solution)/shard_map/while/body/eval_jaxpr/reduce_scatter | solution.py:250
  1133.5 27.4 %reduce-scatter.15.cloned.1.call-done = f32[128,256]{0,1:T(8,128)} async-done(((f32[1024,256]{0,1:T(8,128)}), f32[128,256]{0,1:T(8,128)}) %reduce-scatter.15.cloned.1.call-update) | async-done | bytes 131088 | tf_op jit(solution)/shard_map/while/body/eval_jaxpr/reduce_scatter | solution.py:247
  1162.5 31.5 %reduce-scatter.17.cloned.1.call-done = f32[128,256]{0,1:T(8,128)} async-done(((f32[1024,256]{0,1:T(8,128)}), f32[128,256]{0,1:T(8,128)}) %reduce-scatter.17.cloned.1.call-update) | async-done | bytes 131088 | tf_op jit(solution)/shard_map/while/body/eval_jaxpr/reduce_scatter | solution.py:250
  1204.6 27.3 %reduce-scatter.15.cloned.1.call-done = f32[128,256]{0,1:T(8,128)} async-done(((f32[1024,256]{0,1:T(8,128)}), f32[128,256]{0,1:T(8,128)}) %reduce-scatter.15.cloned.1.call-update) | async-done | bytes 131088 | tf_op jit(solution)/shard_map/while/body/eval_jaxpr/reduce_scatter | solution.py:247
  1233.4 31.4 %reduce-scatter.17.cloned.1.call-done = f32[128,256]{0,1:T(8,128)} async-done(((f32[1024,256]{0,1:T(8,128)}), f32[128,256]{0,1:T(8,128)}) %reduce-scatter.17.cloned.1.call-update) | async-done | bytes 131088 | tf_op jit(solution)/shard_map/while/body/eval_jaxpr/reduce_scatter | solution.py:250
  1268.5 21.6 fusion.40
  1290.2 8.5 fusion.51
  1298.7 5.4 fusion.52
  1304.1 4.9 fusion.50
  1309.0 127.0 %reduce-scatter.13.cloned.1.call-done = f32[256,2048]{1,0:T(8,128)} async-done(((f32[2048,2048]{1,0:T(8,128)}), f32[256,2048]{1,0:T(8,128)}) %reduce-scatter.13.cloned.1.call-update) | async-done | bytes 2097168 | tf_op jit(solution)/shard_map/reduce_scatter | solution.py:287
  1436.0 483.8 %reduce-scatter.11.cloned.1.call-done = f32[2048,768]{1,0:T(8,128)} async-done(((f32[2048,6144]{1,0:T(8,128)}), f32[2048,768]{1,0:T(8,128)}) %reduce-scatter.11.cloned.1.call-update) | async-done | bytes 6291472 | tf_op jit(solution)/shard_map/reduce_scatter | solution.py:285
  1922.8 20.7 fusion.30
  1943.5 26.4 %all-reduce.5 = (f32[2048]{0:T(1024)S(1)}, f32[2048]{0:T(1024)S(1)}, f32[6144]{0:T(1024)S(1)}, f32[2048]{0:T(1024)S(1)}, f32[2048]{0:T(1024)S(1)}) all-reduce(f32[2048]{0:T(1024)S(1)} %get-tuple-element.455, f32[2048]{0:T(1024)S(1)} %get-tuple-element.460, ...), channel_id=6, replica_groups=mesh['row'=4,'seq'=8] {'seq'}, use_global_device_ids=true, to_apply=%region_22.23.clone | all-reduce | flops 14336 | bytes 114688
  1970.3 11.5 all-reduce.6
  1984.4 389.3 %all-reduce.10.cloned.1.call-done = (f32[2048,768]{1,0:T(8,128)}, f32[256,2048]{1,0:T(8,128)}, f32[2048,704]{0,1:T(8,128)}, f32[2048,704]{0,1:T(8,128)}, f32[704,2048]{1,0:T(8,128)}) async-done(((f32[2048,768]{1,0:T(8,128)}, f32[256,2048]{1,0:T(8,128)}, f32[2048,704]{0,1:T(8,128)}, f32[2048,704]{0,1:T(8,128)}, f32[704,2048]{1,0:T(8,128)}), (f32[2048,768]{1,0:T(8,128)}, f32[256,2048]{1,0:T(8,128)}, ...) | async-done | bytes 25690128 | tf_op jit(solution)/shard_map/psum | solution.py:291
  2373.8 6.5 copy.92
  (436 shorter events, 192.7 us)
Async XLA Ops:
  7.2 513.8 %copy-start = (bf16[704,2048]{1,0:T(8,128)(2,1)S(1)}, bf16[704,2048]{1,0:T(8,128)(2,1)}, u32[]{:S(2)}) copy-start(bf16[704,2048]{1,0:T(8,128)(2,1)} %param.30) | copy-start | bytes 8650756
  7.2 16.7 copy-start.18
  7.2 16.7 copy-start.19
  7.2 16.7 copy-start.5
  7.2 225.0 %all-gather.8.cloned.1.call-start = ((), (), s32[]{:S(2)}) async-start(), calls=%async_computation.6 | async-start | bytes 28311552 | tf_op jit(solution)/shard_map/all_gather | solution.py:111
  8.0 282.2 %all-gather.10.cloned.1.call-start = ((), (), s32[]{:S(2)}) async-start(), calls=%async_computation.7 | async-start | bytes 4718592 | tf_op jit(solution)/shard_map/all_gather | solution.py:132
  232.3 12.7 copy-start.29
  244.9 94.0 %all-gather.12.cloned.1.call-start = ((), (), s32[]{:S(2)}) async-start(), calls=%async_computation.8 | async-start | bytes 4718592 | tf_op jit(solution)/shard_map/all_gather | solution.py:131
  257.2 163.4 %all-gather.14.cloned.1.call-start = ((), (), s32[]{:S(2)}) async-start(), calls=%async_computation.9 | async-start | bytes 9437184 | tf_op jit(solution)/shard_map/all_gather | solution.py:112
  257.8 215.4 %all-gather.16.cloned.1.call-start = ((), (), s32[]{:S(2)}) async-start(), calls=%async_computation.10 | async-start | bytes 4718592 | tf_op jit(solution)/shard_map/all_gather | solution.py:179
  427.7 93.3 %all-gather.18.cloned.1.call-start = ((), (), s32[]{:S(2)}) async-start(), calls=%async_computation.12 | async-start | bytes 4718592 | tf_op jit(solution)/shard_map/all_gather | solution.py:194
  431.4 196.3 %reduce-scatter.9.cloned.1.call-start = ((), (), s32[]{:S(2)}) async-start(), calls=%async_computation.13 | async-start | bytes 9437184 | tf_op jit(solution)/shard_map/reduce_scatter | solution.py:202
  473.3 8.0 copy-start.27
  521.0 8.6 copy-start.26
  539.2 139.8 %reduce-scatter.7.cloned.1.call-start = ((), (), s32[]{:S(2)}) async-start(), calls=%async_computation.11 | async-start | bytes 4718592 | tf_op jit(solution)/shard_map/reduce_scatter | solution.py:185
  545.8 81.8 %copy-start.4 = (f32[128,2048]{1,0:T(8,128)S(1)}, f32[128,2048]{1,0:T(8,128)}, u32[]{:S(2)}) copy-start(f32[128,2048]{1,0:T(8,128)} %copy-done.3) | copy-start | bytes 3145732
  681.7 9.5 copy-start.7
  699.6 36.6 %reduce-scatter.15.cloned.1.call-start = ((), (), s32[]{:S(2)}) async-start(), calls=%async_computation.17 | async-start | bytes 1179648 | tf_op jit(solution)/shard_map/while/body/eval_jaxpr/reduce_scatter | solution.py:247
  705.0 64.1 %reduce-scatter.17.cloned.1.call-start = ((), (), s32[]{:S(2)}) async-start(), calls=%async_computation.18 | async-start | bytes 1179648 | tf_op jit(solution)/shard_map/while/body/eval_jaxpr/reduce_scatter | solution.py:250
  706.3 64.4 %copy-start.17 = (bf16[128,2048]{1,0:T(8,128)(2,1)S(1)}, bf16[128,2048]{1,0:T(8,128)(2,1)}, u32[]{:S(2)}) copy-start(bf16[128,2048]{1,0:T(8,128)(2,1)} %copy-done.16) | copy-start | bytes 1572868 | tf_op jit(solution)/shard_map/while
  770.6 36.4 %reduce-scatter.15.cloned.1.call-start = ((), (), s32[]{:S(2)}) async-start(), calls=%async_computation.17 | async-start | bytes 1179648 | tf_op jit(solution)/shard_map/while/body/eval_jaxpr/reduce_scatter | solution.py:247
  776.0 63.8 %reduce-scatter.17.cloned.1.call-start = ((), (), s32[]{:S(2)}) async-start(), calls=%async_computation.18 | async-start | bytes 1179648 | tf_op jit(solution)/shard_map/while/body/eval_jaxpr/reduce_scatter | solution.py:250
  777.4 64.1 %copy-start.17 = (bf16[128,2048]{1,0:T(8,128)(2,1)S(1)}, bf16[128,2048]{1,0:T(8,128)(2,1)}, u32[]{:S(2)}) copy-start(bf16[128,2048]{1,0:T(8,128)(2,1)} %copy-done.16) | copy-start | bytes 1572868 | tf_op jit(solution)/shard_map/while
  841.4 36.3 %reduce-scatter.15.cloned.1.call-start = ((), (), s32[]{:S(2)}) async-start(), calls=%async_computation.17 | async-start | bytes 1179648 | tf_op jit(solution)/shard_map/while/body/eval_jaxpr/reduce_scatter | solution.py:247
  846.8 63.8 %reduce-scatter.17.cloned.1.call-start = ((), (), s32[]{:S(2)}) async-start(), calls=%async_computation.18 | async-start | bytes 1179648 | tf_op jit(solution)/shard_map/while/body/eval_jaxpr/reduce_scatter | solution.py:250
  848.1 64.1 %copy-start.17 = (bf16[128,2048]{1,0:T(8,128)(2,1)S(1)}, bf16[128,2048]{1,0:T(8,128)(2,1)}, u32[]{:S(2)}) copy-start(bf16[128,2048]{1,0:T(8,128)(2,1)} %copy-done.16) | copy-start | bytes 1572868 | tf_op jit(solution)/shard_map/while
  912.2 36.3 %reduce-scatter.15.cloned.1.call-start = ((), (), s32[]{:S(2)}) async-start(), calls=%async_computation.17 | async-start | bytes 1179648 | tf_op jit(solution)/shard_map/while/body/eval_jaxpr/reduce_scatter | solution.py:247
  917.6 63.8 %reduce-scatter.17.cloned.1.call-start = ((), (), s32[]{:S(2)}) async-start(), calls=%async_computation.18 | async-start | bytes 1179648 | tf_op jit(solution)/shard_map/while/body/eval_jaxpr/reduce_scatter | solution.py:250
  918.9 64.0 %copy-start.17 = (bf16[128,2048]{1,0:T(8,128)(2,1)S(1)}, bf16[128,2048]{1,0:T(8,128)(2,1)}, u32[]{:S(2)}) copy-start(bf16[128,2048]{1,0:T(8,128)(2,1)} %copy-done.16) | copy-start | bytes 1572868 | tf_op jit(solution)/shard_map/while
  983.0 36.3 %reduce-scatter.15.cloned.1.call-start = ((), (), s32[]{:S(2)}) async-start(), calls=%async_computation.17 | async-start | bytes 1179648 | tf_op jit(solution)/shard_map/while/body/eval_jaxpr/reduce_scatter | solution.py:247
  988.4 63.8 %reduce-scatter.17.cloned.1.call-start = ((), (), s32[]{:S(2)}) async-start(), calls=%async_computation.18 | async-start | bytes 1179648 | tf_op jit(solution)/shard_map/while/body/eval_jaxpr/reduce_scatter | solution.py:250
  989.7 64.1 %copy-start.17 = (bf16[128,2048]{1,0:T(8,128)(2,1)S(1)}, bf16[128,2048]{1,0:T(8,128)(2,1)}, u32[]{:S(2)}) copy-start(bf16[128,2048]{1,0:T(8,128)(2,1)} %copy-done.16) | copy-start | bytes 1572868 | tf_op jit(solution)/shard_map/while
  1053.8 36.4 %reduce-scatter.15.cloned.1.call-start = ((), (), s32[]{:S(2)}) async-start(), calls=%async_computation.17 | async-start | bytes 1179648 | tf_op jit(solution)/shard_map/while/body/eval_jaxpr/reduce_scatter | solution.py:247
  1059.1 63.9 %reduce-scatter.17.cloned.1.call-start = ((), (), s32[]{:S(2)}) async-start(), calls=%async_computation.18 | async-start | bytes 1179648 | tf_op jit(solution)/shard_map/while/body/eval_jaxpr/reduce_scatter | solution.py:250
  1060.5 64.1 %copy-start.17 = (bf16[128,2048]{1,0:T(8,128)(2,1)S(1)}, bf16[128,2048]{1,0:T(8,128)(2,1)}, u32[]{:S(2)}) copy-start(bf16[128,2048]{1,0:T(8,128)(2,1)} %copy-done.16) | copy-start | bytes 1572868 | tf_op jit(solution)/shard_map/while
  1124.6 36.4 %reduce-scatter.15.cloned.1.call-start = ((), (), s32[]{:S(2)}) async-start(), calls=%async_computation.17 | async-start | bytes 1179648 | tf_op jit(solution)/shard_map/while/body/eval_jaxpr/reduce_scatter | solution.py:247
  1130.0 64.1 %reduce-scatter.17.cloned.1.call-start = ((), (), s32[]{:S(2)}) async-start(), calls=%async_computation.18 | async-start | bytes 1179648 | tf_op jit(solution)/shard_map/while/body/eval_jaxpr/reduce_scatter | solution.py:250
  1131.3 64.3 %copy-start.17 = (bf16[128,2048]{1,0:T(8,128)(2,1)S(1)}, bf16[128,2048]{1,0:T(8,128)(2,1)}, u32[]{:S(2)}) copy-start(bf16[128,2048]{1,0:T(8,128)(2,1)} %copy-done.16) | copy-start | bytes 1572868 | tf_op jit(solution)/shard_map/while
  1195.6 36.3 %reduce-scatter.15.cloned.1.call-start = ((), (), s32[]{:S(2)}) async-start(), calls=%async_computation.17 | async-start | bytes 1179648 | tf_op jit(solution)/shard_map/while/body/eval_jaxpr/reduce_scatter | solution.py:247
  1201.0 63.9 %reduce-scatter.17.cloned.1.call-start = ((), (), s32[]{:S(2)}) async-start(), calls=%async_computation.18 | async-start | bytes 1179648 | tf_op jit(solution)/shard_map/while/body/eval_jaxpr/reduce_scatter | solution.py:250
  1202.3 64.1 %copy-start.17 = (bf16[128,2048]{1,0:T(8,128)(2,1)S(1)}, bf16[128,2048]{1,0:T(8,128)(2,1)}, u32[]{:S(2)}) copy-start(bf16[128,2048]{1,0:T(8,128)(2,1)} %copy-done.16) | copy-start | bytes 1572868 | tf_op jit(solution)/shard_map/while
  1266.4 169.6 %reduce-scatter.13.cloned.1.call-start = ((), (), s32[]{:S(2)}) async-start(), calls=%async_computation.15 | async-start | bytes 18874368 | tf_op jit(solution)/shard_map/reduce_scatter | solution.py:287
  1267.2 652.6 %reduce-scatter.11.cloned.1.call-start = ((), (), s32[]{:S(2)}) async-start(), calls=%async_computation.14 | async-start | bytes 56623104 | tf_op jit(solution)/shard_map/reduce_scatter | solution.py:285
  1290.1 1083.6 %all-reduce.10.cloned.1.call-start = ((), (), s32[]{:S(2)}) async-start(), calls=%async_computation.16 | async-start | bytes 51380224 | tf_op jit(solution)/shard_map/psum | solution.py:291
  1290.2 8.5 copy-start.24
  1290.2 8.5 copy-start.33
  1922.8 59.0 %copy-start.8 = (f32[128,2048]{1,0:T(8,128)S(1)}, f32[128,2048]{1,0:T(8,128)}, u32[]{:S(2)}) copy-start(f32[128,2048]{1,0:T(8,128)} %copy-done.7) | copy-start | bytes 3145732
  2373.8 10.8 slice-start.2
  (40 other events, 124.6 us)
Sparse Core Ops, SparseCore 0:
  9.7 222.5 all-gather.7
  245.1 45.0 all-gather.9
  292.3 46.6 all-gather.11
  340.4 80.2 all-gather.13
  427.8 45.3 all-gather.15
  475.3 45.6 all-gather.17
  539.3 88.3 reduce-scatter.8
  630.5 48.4 reduce-scatter.6
  705.1 31.0 reduce-scatter.14
  738.3 30.7 reduce-scatter.16
  776.2 30.7 reduce-scatter.14
  809.1 30.7 reduce-scatter.16
  846.9 30.7 reduce-scatter.14
  879.9 30.7 reduce-scatter.16
  917.7 30.7 reduce-scatter.14
  950.6 30.7 reduce-scatter.16
  988.5 30.7 reduce-scatter.14
  1021.4 30.7 reduce-scatter.16
  1059.3 30.7 reduce-scatter.14
  1092.2 30.7 reduce-scatter.16
  1130.1 30.7 reduce-scatter.14
  1163.2 30.7 reduce-scatter.16
  1201.1 30.7 reduce-scatter.14
  1234.0 30.7 reduce-scatter.16
  1269.5 166.3 reduce-scatter.12
  1438.2 481.5 reduce-scatter.10
  1924.5 449.1 all-reduce.9
where the time goes:
time: 2410 us; the launch traced here: 2400 us
  waiting for transfers between devices  2000 us (83%)
  matrix products  184 us (8%)
  local copies, waits for them, and re-layouts  117 us (5%)
  blocking collectives  53.7 us (2%)
  other arithmetic  26.4 us (1%)
    reduce_scatter x1, waiting for transfers between devices, body(): lax.psum_scatter(grad_w_qkv, 'seq', scatter_dimension=1, tiled=True)  484 us
    psum x1, waiting for transfers between devices, body(): lax.psum((seq_sums[0], seq_sums[1], seq_sums[2], seq_sums[3], seq_sums[4]...  389 us
    reduce_scatter x8, waiting for transfers between devices, attend_back(): lax.psum_scatter(grad_values.reshape(length, group_width), 'seq', scatter...  251 us
    reduce_scatter x8, waiting for transfers between devices, attend_back(): lax.psum_scatter(grad_keys.reshape(length, group_width), 'seq', scatter_d...  219 us
    all_gather x1, waiting for transfers between devices, body(): lax.all_gather(w_qkv, 'seq', axis=1, tiled=True)  208 us
    reduce_scatter x1, waiting for transfers between devices, body(): lax.psum_scatter(grad_w_out, 'seq', scatter_dimension=0, tiled=True)  127 us
    reduce_scatter x1, waiting for transfers between devices, body(): lax.psum_scatter(right_outer(grad_gate, w_gate) + right_outer(grad_upward...  81.8 us
    dot_general x5, matrix products, left_outer(): lax.dot_general(left, right, (((0,), (0,)), ((), ())), preferred_element_...  49.9 us
  transfers between devices with their start and end apart: 27, of which 27 were waited for; matrix products, arithmetic and copies ran while one was open for 8% of the time, Pallas kernels for 0%

commit v1 on v0

--- a/solution.py
+++ b/solution.py
@@ -9,6 +9,27 @@
 EPS = 1e-05
 NEG = -1e30
 BASE = 10000.0
+
+
+def gather_around(x, axis, dim):
+    count, position, span = (lax.axis_size(axis), lax.axis_index(axis), x.shape[dim])
+    forward = [(i, (i + 1) % count) for i in range(count)]
+    behind = [(i, (i - 1) % count) for i in range(count)]
+    out = jnp.zeros((*x.shape[:dim], count * span, *x.shape[dim + 1 :]), x.dtype)
+    out = lax.dynamic_update_slice_in_dim(out, x, position * span, axis=dim)
+    from_left = from_right = x
+    half = count // 2
+    for step in range(1, half + 1):
+        from_left = lax.ppermute(from_left, axis, forward)
+        out = lax.dynamic_update_slice_in_dim(
+            out, from_left, (position - step) % count * span, axis=dim
+        )
+        if step < count - half:
+            from_right = lax.ppermute(from_right, axis, behind)
+            out = lax.dynamic_update_slice_in_dim(
+                out, from_right, (position + step) % count * span, axis=dim
+            )
+    return out
 
 
 def rotate(tensor, places, direction):
@@ -108,7 +129,7 @@
     normed_one, inverse_one = standardize(tokens)
     first_in = (normed_one * gain_one + shift_one).astype(jnp.bfloat16)
     qkv_full, out_full, bias_full = (
-        lax.all_gather(w_qkv, "seq", axis=1, tiled=True),
+        gather_around(w_qkv, "seq", 1),
         lax.all_gather(w_out, "seq", axis=0, tiled=True),
         lax.all_gather(b_qkv, "seq", axis=0, tiled=True),
     )

time: 2410 us -> 2490 us (1.033)
  local copies, waits for them, and re-layouts: 117 us -> 154 us
  blocking collectives: 53.7 us -> 87.5 us
    all_gather x1 -> x0, waiting for transfers between devices: 208 us -> none  [body(): lax.all_gather(w_qkv, 'seq', axis=1, tiled=True)]
    ppermute x0 -> x7, waiting for transfers between devices: none -> 195 us  [the longest x4 194 us: gather_around(): from_left = lax.ppermute(from_left, axis, forward)]
    all_gather x1, blocking collectives: 15.8 us -> 49.6 us  [body(): lax.all_gather(b_qkv, 'seq', axis=0, tiled=True)]
  transfers between devices with their start and end apart: 27 -> 33, of which waited for: 27 -> 30; matrix products, arithmetic and copies ran while one was open for 8% -> 9% of each run, Pallas kernels for 0% -> 0%
where the time goes in v1:
time: 2490 us; the launch traced here: 2480 us
  waiting for transfers between devices  1990 us (80%)
  matrix products  188 us (8%)
  local copies, waits for them, and re-layouts  154 us (6%)
  blocking collectives  87.5 us (4%)
  other arithmetic  29.1 us (1%)
    reduce_scatter x1, waiting for transfers between devices, body(): lax.psum_scatter(grad_w_qkv, 'seq', scatter_dimension=1, tiled=True)  484 us
    psum x1, waiting for transfers between devices, body(): lax.psum((seq_sums[0], seq_sums[1], seq_sums[2], seq_sums[3], seq_sums[4]...  389 us
    reduce_scatter x8, waiting for transfers between devices, attend_back(): lax.psum_scatter(grad_values.reshape(length, group_width), 'seq', scatter...  252 us
    reduce_scatter x8, waiting for transfers between devices, attend_back(): lax.psum_scatter(grad_keys.reshape(length, group_width), 'seq', scatter_d...  218 us
    ppermute x4, waiting for transfers between devices, gather_around(): from_left = lax.ppermute(from_left, axis, forward)  194 us
    reduce_scatter x1, waiting for transfers between devices, body(): lax.psum_scatter(grad_w_out, 'seq', scatter_dimension=0, tiled=True)  127 us
    reduce_scatter x1, waiting for transfers between devices, body(): lax.psum_scatter(right_outer(grad_gate, w_gate) + right_outer(grad_upward...  81.8 us
  transfers between devices with their start and end apart: 33, of which 30 were waited for; matrix products, arithmetic and copies ran while one was open for 9% of the time, Pallas kernels for 0%

profile of v1, /device:TPU:0, one launch (start us, length us, event | category | flops | bytes accessed | tf_op | source)
XLA Modules:
  0.0 2476.8 jit_solution(18127959643612547090)
XLA Ops:
  11.9 66.2 %collective-permute-done = bf16[2048,768]{1,0:T(8,128)(2,1)S(1)} collective-permute-done((bf16[2048,768]{1,0:T(8,128)(2,1)}, bf16[2048,768]{1,0:T(8,128)(2,1)S(1)}, u32[]{:S(2)}, u32[]{:S(2)}) %collective-permute-start) | collective-permute-done | bytes 3145760 | tf_op jit(solution)/shard_map/ppermute | solution.py:23
  83.3 65.3 %collective-permute-done.2 = bf16[2048,768]{1,0:T(8,128)(2,1)S(1)} collective-permute-done((bf16[2048,768]{1,0:T(8,128)(2,1)S(1)}, bf16[2048,768]{1,0:T(8,128)(2,1)S(1)}, u32[]{:S(2)}, u32[]{:S(2)}) %collective-permute-start.2) | collective-permute-done | bytes 3145760 | tf_op jit(solution)/shard_map/ppermute | solution.py:23
  152.7 63.0 %collective-permute-done.4 = bf16[2048,768]{1,0:T(8,128)(2,1)} collective-permute-done((bf16[2048,768]{1,0:T(8,128)(2,1)S(1)}, bf16[2048,768]{1,0:T(8,128)(2,1)}, u32[]{:S(2)}, u32[]{:S(2)}) %collective-permute-start.4) | collective-permute-done | bytes 3145760 | tf_op jit(solution)/shard_map/ppermute | solution.py:23
  216.4 49.6 %all-gather = bf16[8,1,768]{2,1,0:T(2,128)(2,1)S(1)} all-gather(bf16[1,1,768]{2,1,0:T(2,128)(2,1)S(1)} %reshape.337), channel_id=1, replica_groups=mesh['row'=4,'seq'=8] {'seq'}, dimensions={0}, use_global_device_ids=true | all-gather | bytes 13824 | tf_op jit(solution)/shard_map/all_gather | solution.py:134
  270.0 8.8 broadcast_in_dim.118
  305.3 13.4 convolution_add_fusion
  338.8 29.4 %all-gather.7.cloned.1.call-done = bf16[1024,2048]{1,0:T(8,128)(2,1)} async-done(((bf16[128,2048]{1,0:T(8,128)(2,1)}), bf16[1024,2048]{1,0:T(8,128)(2,1)}) %all-gather.7.cloned.1.call-update) | async-done | bytes 4194320 | tf_op jit(solution)/shard_map/all_gather | solution.py:153
  368.2 6.4 copy.55
  374.6 42.4 %all-gather.9.cloned.1.call-done = bf16[1024,2048]{0,1:T(8,128)(2,1)} async-done(((bf16[128,2048]{0,1:T(8,128)(2,1)}), bf16[1024,2048]{0,1:T(8,128)(2,1)}) %all-gather.9.cloned.1.call-update) | async-done | bytes 4194320 | tf_op jit(solution)/shard_map/all_gather | solution.py:152
  417.0 39.6 %while.34 = (s32[]{:T(128)}, bf16[128,2048]{0,1:T(8,128)(2,1)}, f32[32,128]{1,0:T(8,128)S(1)}, bf16[1024,2048]{0,1:T(8,128)(2,1)}, bf16[128,2048]{0,1:T(8,128)(2...) while((s32[]{:T(128)}, bf16[128,2048]{0,1:T(8,128)(2,1)}, ...), condition=%wide.region_5.6_spmd.clone, body=%wide.region_2.5_spmd.clone.sunk | while | flops 140639872 | bytes 10372341 | solution.py:187
  456.7 42.2 %all-gather.11.cloned.1.call-done = bf16[2048,2048]{1,0:T(8,128)(2,1)} async-done(((bf16[256,2048]{1,0:T(8,128)(2,1)}), bf16[2048,2048]{1,0:T(8,128)(2,1)}) %all-gather.11.cloned.1.call-update) | async-done | bytes 8388624 | tf_op jit(solution)/shard_map/all_gather | solution.py:133
  509.6 41.8 %all-gather.13.cloned.1.call-done = bf16[1024,2048]{1,0:T(8,128)(2,1)} async-done(((bf16[128,2048]{1,0:T(8,128)(2,1)}), bf16[1024,2048]{1,0:T(8,128)(2,1)}) %all-gather.13.cloned.1.call-update) | async-done | bytes 4194320 | tf_op jit(solution)/shard_map/all_gather | solution.py:200
  551.5 8.0 fusion.47
  564.2 35.0 %all-gather.15.cloned.1.call-done = bf16[1024,2048]{1,0:T(8,128)(2,1)} async-done(((bf16[128,2048]{1,0:T(8,128)(2,1)}), bf16[1024,2048]{1,0:T(8,128)(2,1)}) %all-gather.15.cloned.1.call-update) | async-done | bytes 4194320 | tf_op jit(solution)/shard_map/all_gather | solution.py:215
  599.2 8.6 multiply_convert_fusion.1
  611.4 6.0 convolution_add_fusion.1
  617.5 6.6 convolution_convert_fusion
  624.2 81.8 %reduce-scatter.9.cloned.1.call-done = f32[128,2048]{1,0:T(8,128)} async-done(((f32[1024,2048]{1,0:T(8,128)}), f32[128,2048]{1,0:T(8,128)}) %reduce-scatter.9.cloned.1.call-update) | async-done | bytes 1048592 | tf_op jit(solution)/shard_map/reduce_scatter | solution.py:223
  707.6 49.6 %reduce-scatter.7.cloned.1.call-done = bf16[128,2048]{1,0:T(8,128)(2,1)} async-done(((bf16[1024,2048]{1,0:T(8,128)(2,1)}), bf16[128,2048]{1,0:T(8,128)(2,1)}) %reduce-scatter.7.cloned.1.call-update) | async-done | bytes 524304 | tf_op jit(solution)/shard_map/reduce_scatter | solution.py:206
  759.9 9.5 fusion.34
  769.4 6.3 convolution_convert_fusion.1
  777.8 567.7 %while.35 = (s32[]{:T(128)}, f32[128,2048]{0,1:T(8,128)}, f32[128,2048]{0,1:T(8,128)}, bf16[128,2048]{0,1:T(8,128)(2,1)}, bf16[1024,2048]{0,1:T(8,128)(2,1)}, /*...) while((s32[]{:T(128)}, f32[128,2048]{0,1:T(8,128)}, ...), condition=%wide.region_18.19_spmd.clone, body=%wide.region_14.0_spmd.clone.sunk | while | flops 340688512 | bytes 36711860 | solution.py:283
  786.8 27.5 %reduce-scatter.15.cloned.1.call-done = f32[128,256]{0,1:T(8,128)} async-done(((f32[1024,256]{0,1:T(8,128)}), f32[128,256]{0,1:T(8,128)}) %reduce-scatter.15.cloned.1.call-update) | async-done | bytes 131088 | tf_op jit(solution)/shard_map/while/body/eval_jaxpr/reduce_scatter | solution.py:268
  815.9 31.5 %reduce-scatter.17.cloned.1.call-done = f32[128,256]{0,1:T(8,128)} async-done(((f32[1024,256]{0,1:T(8,128)}), f32[128,256]{0,1:T(8,128)}) %reduce-scatter.17.cloned.1.call-update) | async-done | bytes 131088 | tf_op jit(solution)/shard_map/while/body/eval_jaxpr/reduce_scatter | solution.py:271
  858.1 27.2 %reduce-scatter.15.cloned.1.call-done = f32[128,256]{0,1:T(8,128)} async-done(((f32[1024,256]{0,1:T(8,128)}), f32[128,256]{0,1:T(8,128)}) %reduce-scatter.15.cloned.1.call-update) | async-done | bytes 131088 | tf_op jit(solution)/shard_map/while/body/eval_jaxpr/reduce_scatter | solution.py:268
  886.8 31.5 %reduce-scatter.17.cloned.1.call-done = f32[128,256]{0,1:T(8,128)} async-done(((f32[1024,256]{0,1:T(8,128)}), f32[128,256]{0,1:T(8,128)}) %reduce-scatter.17.cloned.1.call-update) | async-done | bytes 131088 | tf_op jit(solution)/shard_map/while/body/eval_jaxpr/reduce_scatter | solution.py:271
  929.0 27.3 %reduce-scatter.15.cloned.1.call-done = f32[128,256]{0,1:T(8,128)} async-done(((f32[1024,256]{0,1:T(8,128)}), f32[128,256]{0,1:T(8,128)}) %reduce-scatter.15.cloned.1.call-update) | async-done | bytes 131088 | tf_op jit(solution)/shard_map/while/body/eval_jaxpr/reduce_scatter | solution.py:268
  957.8 31.6 %reduce-scatter.17.cloned.1.call-done = f32[128,256]{0,1:T(8,128)} async-done(((f32[1024,256]{0,1:T(8,128)}), f32[128,256]{0,1:T(8,128)}) %reduce-scatter.17.cloned.1.call-update) | async-done | bytes 131088 | tf_op jit(solution)/shard_map/while/body/eval_jaxpr/reduce_scatter | solution.py:271
  1000.0 27.3 %reduce-scatter.15.cloned.1.call-done = f32[128,256]{0,1:T(8,128)} async-done(((f32[1024,256]{0,1:T(8,128)}), f32[128,256]{0,1:T(8,128)}) %reduce-scatter.15.cloned.1.call-update) | async-done | bytes 131088 | tf_op jit(solution)/shard_map/while/body/eval_jaxpr/reduce_scatter | solution.py:268
  1028.8 31.3 %reduce-scatter.17.cloned.1.call-done = f32[128,256]{0,1:T(8,128)} async-done(((f32[1024,256]{0,1:T(8,128)}), f32[128,256]{0,1:T(8,128)}) %reduce-scatter.17.cloned.1.call-update) | async-done | bytes 131088 | tf_op jit(solution)/shard_map/while/body/eval_jaxpr/reduce_scatter | solution.py:271
  1070.7 27.3 %reduce-scatter.15.cloned.1.call-done = f32[128,256]{0,1:T(8,128)} async-done(((f32[1024,256]{0,1:T(8,128)}), f32[128,256]{0,1:T(8,128)}) %reduce-scatter.15.cloned.1.call-update) | async-done | bytes 131088 | tf_op jit(solution)/shard_map/while/body/eval_jaxpr/reduce_scatter | solution.py:268
  1099.5 31.4 %reduce-scatter.17.cloned.1.call-done = f32[128,256]{0,1:T(8,128)} async-done(((f32[1024,256]{0,1:T(8,128)}), f32[128,256]{0,1:T(8,128)}) %reduce-scatter.17.cloned.1.call-update) | async-done | bytes 131088 | tf_op jit(solution)/shard_map/while/body/eval_jaxpr/reduce_scatter | solution.py:271
  1141.6 27.2 %reduce-scatter.15.cloned.1.call-done = f32[128,256]{0,1:T(8,128)} async-done(((f32[1024,256]{0,1:T(8,128)}), f32[128,256]{0,1:T(8,128)}) %reduce-scatter.15.cloned.1.call-update) | async-done | bytes 131088 | tf_op jit(solution)/shard_map/while/body/eval_jaxpr/reduce_scatter | solution.py:268
  1170.3 31.5 %reduce-scatter.17.cloned.1.call-done = f32[128,256]{0,1:T(8,128)} async-done(((f32[1024,256]{0,1:T(8,128)}), f32[128,256]{0,1:T(8,128)}) %reduce-scatter.17.cloned.1.call-update) | async-done | bytes 131088 | tf_op jit(solution)/shard_map/while/body/eval_jaxpr/reduce_scatter | solution.py:271
  1212.5 27.3 %reduce-scatter.15.cloned.1.call-done = f32[128,256]{0,1:T(8,128)} async-done(((f32[1024,256]{0,1:T(8,128)}), f32[128,256]{0,1:T(8,128)}) %reduce-scatter.15.cloned.1.call-update) | async-done | bytes 131088 | tf_op jit(solution)/shard_map/while/body/eval_jaxpr/reduce_scatter | solution.py:268
  1241.3 31.6 %reduce-scatter.17.cloned.1.call-done = f32[128,256]{0,1:T(8,128)} async-done(((f32[1024,256]{0,1:T(8,128)}), f32[128,256]{0,1:T(8,128)}) %reduce-scatter.17.cloned.1.call-update) | async-done | bytes 131088 | tf_op jit(solution)/shard_map/while/body/eval_jaxpr/reduce_scatter | solution.py:271
  1283.4 27.4 %reduce-scatter.15.cloned.1.call-done = f32[128,256]{0,1:T(8,128)} async-done(((f32[1024,256]{0,1:T(8,128)}), f32[128,256]{0,1:T(8,128)}) %reduce-scatter.15.cloned.1.call-update) | async-done | bytes 131088 | tf_op jit(solution)/shard_map/while/body/eval_jaxpr/reduce_scatter | solution.py:268
  1312.4 31.5 %reduce-scatter.17.cloned.1.call-done = f32[128,256]{0,1:T(8,128)} async-done(((f32[1024,256]{0,1:T(8,128)}), f32[128,256]{0,1:T(8,128)}) %reduce-scatter.17.cloned.1.call-update) | async-done | bytes 131088 | tf_op jit(solution)/shard_map/while/body/eval_jaxpr/reduce_scatter | solution.py:271
  1347.5 21.6 fusion.40
  1369.2 8.5 fusion.51
  1377.7 5.1 fusion.52
  1387.8 126.9 %reduce-scatter.13.cloned.1.call-done = f32[256,2048]{1,0:T(8,128)} async-done(((f32[2048,2048]{1,0:T(8,128)}), f32[256,2048]{1,0:T(8,128)}) %reduce-scatter.13.cloned.1.call-update) | async-done | bytes 2097168 | tf_op jit(solution)/shard_map/reduce_scatter | solution.py:308
  1514.6 483.9 %reduce-scatter.11.cloned.1.call-done = f32[2048,768]{1,0:T(8,128)} async-done(((f32[2048,6144]{1,0:T(8,128)}), f32[2048,768]{1,0:T(8,128)}) %reduce-scatter.11.cloned.1.call-update) | async-done | bytes 6291472 | tf_op jit(solution)/shard_map/reduce_scatter | solution.py:306
  2001.6 20.7 fusion.30
  2022.3 26.4 %all-reduce.5 = (f32[2048]{0:T(1024)S(1)}, f32[2048]{0:T(1024)S(1)}, f32[6144]{0:T(1024)S(1)}, f32[2048]{0:T(1024)S(1)}, f32[2048]{0:T(1024)S(1)}) all-reduce(f32[2048]{0:T(1024)S(1)} %get-tuple-element.455, f32[2048]{0:T(1024)S(1)} %get-tuple-element.460, ...), channel_id=6, replica_groups=mesh['row'=4,'seq'=8] {'seq'}, use_global_device_ids=true, to_apply=%region_22.23.clone | all-reduce | flops 14336 | bytes 114688
  2049.0 11.5 all-reduce.6
  2063.2 389.3 %all-reduce.10.cloned.1.call-done = (f32[2048,768]{1,0:T(8,128)}, f32[256,2048]{1,0:T(8,128)}, f32[2048,704]{0,1:T(8,128)}, f32[2048,704]{0,1:T(8,128)}, f32[704,2048]{1,0:T(8,128)}) async-done(((f32[2048,768]{1,0:T(8,128)}, f32[256,2048]{1,0:T(8,128)}, f32[2048,704]{0,1:T(8,128)}, f32[2048,704]{0,1:T(8,128)}, f32[704,2048]{1,0:T(8,128)}), (f32[2048,768]{1,0:T(8,128)}, f32[256,2048]{1,0:T(8,128)}, ...) | async-done | bytes 25690128 | tf_op jit(solution)/shard_map/psum | solution.py:312
  2452.5 6.5 copy.100
  (464 shorter events, 248.5 us)
Async XLA Ops:
  7.2 592.0 %copy-start = (bf16[704,2048]{1,0:T(8,128)(2,1)S(1)}, bf16[704,2048]{1,0:T(8,128)(2,1)}, u32[]{:S(2)}) copy-start(bf16[704,2048]{1,0:T(8,128)(2,1)} %param.30) | copy-start | bytes 8650756
  7.2 361.0 %all-gather.7.cloned.1.call-start = ((), (), s32[]{:S(2)}) async-start(), calls=%async_computation.6 | async-start | bytes 4718592 | tf_op jit(solution)/shard_map/all_gather | solution.py:153
  7.2 70.8 %collective-permute-start = (bf16[2048,768]{1,0:T(8,128)(2,1)}, bf16[2048,768]{1,0:T(8,128)(2,1)S(1)}, u32[]{:S(2)}, u32[]{:S(2)}) collective-permute-start(bf16[2048,768]{1,0:T(8,128)(2,1)} %param.23), channel_id=1, source_target_pairs={{0,1},{1,2},{2,3},{3,4},{4,5},{5,6},{6,7},{7,0},{8,9},{9,10},{10,1... | collective-permute-start | bytes 9437192 | tf_op jit(solution)/shard_map/ppermute | solution.py:23
  7.8 72.0 %collective-permute-start.1 = (bf16[2048,768]{1,0:T(8,128)(2,1)}, bf16[2048,768]{1,0:T(8,128)(2,1)S(1)}, u32[]{:S(2)}, u32[]{:S(2)}) collective-permute-start(bf16[2048,768]{1,0:T(8,128)(2,1)} %param.23), channel_id=1, source_target_pairs={{0,7},{1,0},{2,1},{3,2},{4,3},{5,4},{6,5},{7,6},{8,15},{9,8},{10,9... | collective-permute-start | bytes 9437192 | tf_op jit(solution)/shard_map/ppermute | solution.py:28
  79.8 68.8 %collective-permute-start.2 = (bf16[2048,768]{1,0:T(8,128)(2,1)S(1)}, bf16[2048,768]{1,0:T(8,128)(2,1)S(1)}, u32[]{:S(2)}, u32[]{:S(2)}) collective-permute-start(bf16[2048,768]{1,0:T(8,128)(2,1)S(1)} %collective-permute-done), channel_id=1, source_target_pairs={{0,1},{1,2},{2,3},{3,4},{4,5},{5,6},{6,7},{7,0},{8,9},{9,10},{10,1... | collective-permute-start | bytes 9437192 | tf_op jit(solution)/shard_map/ppermute | solution.py:23
  79.8 68.8 %copy-start.15 = (bf16[2048,768]{1,0:T(8,128)(2,1)}, bf16[2048,768]{1,0:T(8,128)(2,1)S(1)}, u32[]{:S(2)}) copy-start(bf16[2048,768]{1,0:T(8,128)(2,1)S(1)} %collective-permute-done.1) | copy-start | bytes 9437188
  79.8 69.1 %collective-permute-start.3 = (bf16[2048,768]{1,0:T(8,128)(2,1)S(1)}, bf16[2048,768]{1,0:T(8,128)(2,1)}, u32[]{:S(2)}, u32[]{:S(2)}) collective-permute-start(bf16[2048,768]{1,0:T(8,128)(2,1)S(1)} %collective-permute-done.1), channel_id=1, source_target_pairs={{0,7},{1,0},{2,1},{3,2},{4,3},{5,4},{6,5},{7,6},{8,15},{9,8},{10,9... | collective-permute-start | bytes 9437192 | tf_op jit(solution)/shard_map/ppermute | solution.py:28
  148.6 67.1 %collective-permute-start.4 = (bf16[2048,768]{1,0:T(8,128)(2,1)S(1)}, bf16[2048,768]{1,0:T(8,128)(2,1)}, u32[]{:S(2)}, u32[]{:S(2)}) collective-permute-start(bf16[2048,768]{1,0:T(8,128)(2,1)S(1)} %collective-permute-done.2), channel_id=1, source_target_pairs={{0,1},{1,2},{2,3},{3,4},{4,5},{5,6},{6,7},{7,0},{8,9},{9,10},{10,1... | collective-permute-start | bytes 9437192 | tf_op jit(solution)/shard_map/ppermute | solution.py:23
  150.2 147.2 %collective-permute-start.5 = (bf16[2048,768]{1,0:T(8,128)(2,1)}, bf16[2048,768]{1,0:T(8,128)(2,1)}, u32[]{:S(2)}, u32[]{:S(2)}) collective-permute-start(bf16[2048,768]{1,0:T(8,128)(2,1)} %collective-permute-done.3), channel_id=1, source_target_pairs={{0,7},{1,0},{2,1},{3,2},{4,3},{5,4},{6,5},{7,6},{8,15},{9,8},{10,9... | collective-permute-start | bytes 9437192 | tf_op jit(solution)/shard_map/ppermute | solution.py:28
  215.7 85.7 %collective-permute-start.6 = (bf16[2048,768]{1,0:T(8,128)(2,1)}, bf16[2048,768]{1,0:T(8,128)(2,1)}, u32[]{:S(2)}, u32[]{:S(2)}) collective-permute-start(bf16[2048,768]{1,0:T(8,128)(2,1)} %collective-permute-done.4), channel_id=1, source_target_pairs={{0,1},{1,2},{2,3},{3,4},{4,5},{5,6},{6,7},{7,0},{8,9},{9,10},{10,1... | collective-permute-start | bytes 9437192 | tf_op jit(solution)/shard_map/ppermute | solution.py:23
  305.3 15.6 copy-start.33
  320.8 96.3 %all-gather.9.cloned.1.call-start = ((), (), s32[]{:S(2)}) async-start(), calls=%async_computation.7 | async-start | bytes 4718592 | tf_op jit(solution)/shard_map/all_gather | solution.py:152
  333.3 165.6 %all-gather.11.cloned.1.call-start = ((), (), s32[]{:S(2)}) async-start(), calls=%async_computation.8 | async-start | bytes 9437184 | tf_op jit(solution)/shard_map/all_gather | solution.py:133
  334.0 217.5 %all-gather.13.cloned.1.call-start = ((), (), s32[]{:S(2)}) async-start(), calls=%async_computation.9 | async-start | bytes 4718592 | tf_op jit(solution)/shard_map/all_gather | solution.py:200
  506.0 93.3 %all-gather.15.cloned.1.call-start = ((), (), s32[]{:S(2)}) async-start(), calls=%async_computation.11 | async-start | bytes 4718592 | tf_op jit(solution)/shard_map/all_gather | solution.py:215
  509.6 196.4 %reduce-scatter.9.cloned.1.call-start = ((), (), s32[]{:S(2)}) async-start(), calls=%async_computation.12 | async-start | bytes 9437184 | tf_op jit(solution)/shard_map/reduce_scatter | solution.py:223
  617.4 139.8 %reduce-scatter.7.cloned.1.call-start = ((), (), s32[]{:S(2)}) async-start(), calls=%async_computation.10 | async-start | bytes 4718592 | tf_op jit(solution)/shard_map/reduce_scatter | solution.py:206
  624.1 81.8 %copy-start.4 = (f32[128,2048]{1,0:T(8,128)S(1)}, f32[128,2048]{1,0:T(8,128)}, u32[]{:S(2)}) copy-start(f32[128,2048]{1,0:T(8,128)} %copy-done.3) | copy-start | bytes 3145732
  759.9 9.5 copy-start.7
  777.8 36.6 %reduce-scatter.15.cloned.1.call-start = ((), (), s32[]{:S(2)}) async-start(), calls=%async_computation.16 | async-start | bytes 1179648 | tf_op jit(solution)/shard_map/while/body/eval_jaxpr/reduce_scatter | solution.py:268
  783.2 64.3 %reduce-scatter.17.cloned.1.call-start = ((), (), s32[]{:S(2)}) async-start(), calls=%async_computation.17 | async-start | bytes 1179648 | tf_op jit(solution)/shard_map/while/body/eval_jaxpr/reduce_scatter | solution.py:271
  784.6 64.4 %copy-start.24 = (bf16[128,2048]{1,0:T(8,128)(2,1)S(1)}, bf16[128,2048]{1,0:T(8,128)(2,1)}, u32[]{:S(2)}) copy-start(bf16[128,2048]{1,0:T(8,128)(2,1)} %copy-done.23) | copy-start | bytes 1572868 | tf_op jit(solution)/shard_map/while
  849.0 36.3 %reduce-scatter.15.cloned.1.call-start = ((), (), s32[]{:S(2)}) async-start(), calls=%async_computation.16 | async-start | bytes 1179648 | tf_op jit(solution)/shard_map/while/body/eval_jaxpr/reduce_scatter | solution.py:268
  854.4 64.0 %reduce-scatter.17.cloned.1.call-start = ((), (), s32[]{:S(2)}) async-start(), calls=%async_computation.17 | async-start | bytes 1179648 | tf_op jit(solution)/shard_map/while/body/eval_jaxpr/reduce_scatter | solution.py:271
  855.8 64.1 %copy-start.24 = (bf16[128,2048]{1,0:T(8,128)(2,1)S(1)}, bf16[128,2048]{1,0:T(8,128)(2,1)}, u32[]{:S(2)}) copy-start(bf16[128,2048]{1,0:T(8,128)(2,1)} %copy-done.23) | copy-start | bytes 1572868 | tf_op jit(solution)/shard_map/while
  919.9 36.3 %reduce-scatter.15.cloned.1.call-start = ((), (), s32[]{:S(2)}) async-start(), calls=%async_computation.16 | async-start | bytes 1179648 | tf_op jit(solution)/shard_map/while/body/eval_jaxpr/reduce_scatter | solution.py:268
  925.3 64.1 %reduce-scatter.17.cloned.1.call-start = ((), (), s32[]{:S(2)}) async-start(), calls=%async_computation.17 | async-start | bytes 1179648 | tf_op jit(solution)/shard_map/while/body/eval_jaxpr/reduce_scatter | solution.py:271
  926.7 64.2 %copy-start.24 = (bf16[128,2048]{1,0:T(8,128)(2,1)S(1)}, bf16[128,2048]{1,0:T(8,128)(2,1)}, u32[]{:S(2)}) copy-start(bf16[128,2048]{1,0:T(8,128)(2,1)} %copy-done.23) | copy-start | bytes 1572868 | tf_op jit(solution)/shard_map/while
  990.9 36.3 %reduce-scatter.15.cloned.1.call-start = ((), (), s32[]{:S(2)}) async-start(), calls=%async_computation.16 | async-start | bytes 1179648 | tf_op jit(solution)/shard_map/while/body/eval_jaxpr/reduce_scatter | solution.py:268
  996.3 63.8 %reduce-scatter.17.cloned.1.call-start = ((), (), s32[]{:S(2)}) async-start(), calls=%async_computation.17 | async-start | bytes 1179648 | tf_op jit(solution)/shard_map/while/body/eval_jaxpr/reduce_scatter | solution.py:271
  997.7 64.0 %copy-start.24 = (bf16[128,2048]{1,0:T(8,128)(2,1)S(1)}, bf16[128,2048]{1,0:T(8,128)(2,1)}, u32[]{:S(2)}) copy-start(bf16[128,2048]{1,0:T(8,128)(2,1)} %copy-done.23) | copy-start | bytes 1572868 | tf_op jit(solution)/shard_map/while
  1061.6 36.3 %reduce-scatter.15.cloned.1.call-start = ((), (), s32[]{:S(2)}) async-start(), calls=%async_computation.16 | async-start | bytes 1179648 | tf_op jit(solution)/shard_map/while/body/eval_jaxpr/reduce_scatter | solution.py:268
  1067.0 63.9 %reduce-scatter.17.cloned.1.call-start = ((), (), s32[]{:S(2)}) async-start(), calls=%async_computation.17 | async-start | bytes 1179648 | tf_op jit(solution)/shard_map/while/body/eval_jaxpr/reduce_scatter | solution.py:271
  1068.4 64.1 %copy-start.24 = (bf16[128,2048]{1,0:T(8,128)(2,1)S(1)}, bf16[128,2048]{1,0:T(8,128)(2,1)}, u32[]{:S(2)}) copy-start(bf16[128,2048]{1,0:T(8,128)(2,1)} %copy-done.23) | copy-start | bytes 1572868 | tf_op jit(solution)/shard_map/while
  1132.5 36.3 %reduce-scatter.15.cloned.1.call-start = ((), (), s32[]{:S(2)}) async-start(), calls=%async_computation.16 | async-start | bytes 1179648 | tf_op jit(solution)/shard_map/while/body/eval_jaxpr/reduce_scatter | solution.py:268
  1137.9 64.0 %reduce-scatter.17.cloned.1.call-start = ((), (), s32[]{:S(2)}) async-start(), calls=%async_computation.17 | async-start | bytes 1179648 | tf_op jit(solution)/shard_map/while/body/eval_jaxpr/reduce_scatter | solution.py:271
  1139.3 64.1 %copy-start.24 = (bf16[128,2048]{1,0:T(8,128)(2,1)S(1)}, bf16[128,2048]{1,0:T(8,128)(2,1)}, u32[]{:S(2)}) copy-start(bf16[128,2048]{1,0:T(8,128)(2,1)} %copy-done.23) | copy-start | bytes 1572868 | tf_op jit(solution)/shard_map/while
  1203.4 36.3 %reduce-scatter.15.cloned.1.call-start = ((), (), s32[]{:S(2)}) async-start(), calls=%async_computation.16 | async-start | bytes 1179648 | tf_op jit(solution)/shard_map/while/body/eval_jaxpr/reduce_scatter | solution.py:268
  1208.8 64.1 %reduce-scatter.17.cloned.1.call-start = ((), (), s32[]{:S(2)}) async-start(), calls=%async_computation.17 | async-start | bytes 1179648 | tf_op jit(solution)/shard_map/while/body/eval_jaxpr/reduce_scatter | solution.py:271
  1210.2 64.2 %copy-start.24 = (bf16[128,2048]{1,0:T(8,128)(2,1)S(1)}, bf16[128,2048]{1,0:T(8,128)(2,1)}, u32[]{:S(2)}) copy-start(bf16[128,2048]{1,0:T(8,128)(2,1)} %copy-done.23) | copy-start | bytes 1572868 | tf_op jit(solution)/shard_map/while
  1274.4 36.4 %reduce-scatter.15.cloned.1.call-start = ((), (), s32[]{:S(2)}) async-start(), calls=%async_computation.16 | async-start | bytes 1179648 | tf_op jit(solution)/shard_map/while/body/eval_jaxpr/reduce_scatter | solution.py:268
  1279.8 64.2 %reduce-scatter.17.cloned.1.call-start = ((), (), s32[]{:S(2)}) async-start(), calls=%async_computation.17 | async-start | bytes 1179648 | tf_op jit(solution)/shard_map/while/body/eval_jaxpr/reduce_scatter | solution.py:271
  1281.2 64.3 %copy-start.24 = (bf16[128,2048]{1,0:T(8,128)(2,1)S(1)}, bf16[128,2048]{1,0:T(8,128)(2,1)}, u32[]{:S(2)}) copy-start(bf16[128,2048]{1,0:T(8,128)(2,1)} %copy-done.23) | copy-start | bytes 1572868 | tf_op jit(solution)/shard_map/while
  1345.5 169.1 %reduce-scatter.13.cloned.1.call-start = ((), (), s32[]{:S(2)}) async-start(), calls=%async_computation.14 | async-start | bytes 18874368 | tf_op jit(solution)/shard_map/reduce_scatter | solution.py:308
  1346.1 652.4 %reduce-scatter.11.cloned.1.call-start = ((), (), s32[]{:S(2)}) async-start(), calls=%async_computation.13 | async-start | bytes 56623104 | tf_op jit(solution)/shard_map/reduce_scatter | solution.py:306
  1369.1 1083.4 %all-reduce.10.cloned.1.call-start = ((), (), s32[]{:S(2)}) async-start(), calls=%async_computation.15 | async-start | bytes 51380224 | tf_op jit(solution)/shard_map/psum | solution.py:312
  2001.6 59.0 %copy-start.8 = (f32[128,2048]{1,0:T(8,128)S(1)}, f32[128,2048]{1,0:T(8,128)}, u32[]{:S(2)}) copy-start(f32[128,2048]{1,0:T(8,128)} %copy-done.7) | copy-start | bytes 3145732
  2452.5 10.8 slice-start.2
  (50 other events, 182.2 us)
Sparse Core Ops, SparseCore 0:
  320.9 47.3 all-gather.6
  370.4 46.6 all-gather.8
  418.7 80.2 all-gather.10
  506.1 45.3 all-gather.12
  553.5 45.6 all-gather.14
  617.6 88.3 reduce-scatter.8
  708.8 48.3 reduce-scatter.6
  783.3 31.0 reduce-scatter.14
  816.7 30.7 reduce-scatter.16
  854.5 30.7 reduce-scatter.14
  887.6 30.7 reduce-scatter.16
  925.4 30.7 reduce-scatter.14
  958.5 30.8 reduce-scatter.16
  996.4 30.7 reduce-scatter.14
  1029.3 30.7 reduce-scatter.16
  1067.1 30.7 reduce-scatter.14
  1100.1 30.8 reduce-scatter.16
  1138.0 30.7 reduce-scatter.14
  1171.1 30.7 reduce-scatter.16
  1208.9 30.7 reduce-scatter.14
  1242.0 30.7 reduce-scatter.16
  1279.9 30.9 reduce-scatter.14
  1313.1 30.7 reduce-scatter.16
  1348.4 166.2 reduce-scatter.12
  1517.0 481.4 reduce-scatter.10
  2003.3 449.1 all-reduce.9
